TPU v7x, 32 devices: a whole 2x2x4 slice. The times are simulated.
32 devices in a mesh: pipe: 4 (over y, core), ctx: 4 (over z), dp: 2 (over x).
Axes of the slice: x: 2, y: 2, z: 4, core: 2. Of those that a mesh axis runs over, the one named last changes fastest.
Arguments:
- hidden: bfloat16 [4, 1024, 4096], P('pipe', 'ctx', 'dp'), may hold values from -64 to 64
- cotangent: bfloat16 [4, 1024, 4096], P('pipe', 'ctx', 'dp'), may hold values from -6 to 6
- gain_rows: float32 [4, 4096], P('pipe', ('dp', 'ctx')), may hold values from 0.5 to 1.5
- short_taps: float32 [4, 9, 4096], P('pipe', None, ('dp', 'ctx')), may hold values from -3.5 to 3.5
- long_taps: float32 [4, 7, 4096], P('pipe', None, ('dp', 'ctx')), may hold values from -2 to 2
Outputs:
- hidden_grad: bfloat16 [4, 1024, 4096], P('pipe', 'ctx', 'dp')
- gain_grad: float32 [4, 4096], P('pipe', ('dp', 'ctx'))
- short_grad: float32 [4, 9, 4096], P('pipe', None, ('dp', 'ctx'))
- long_grad: float32 [4, 7, 4096], P('pipe', None, ('dp', 'ctx'))
All inputs are finite; a program needn't handle non-finite values.
Results may differ from a plain program's by a relative error of at most 0.0056.
Values may be sent and summed in bfloat16 or wider, within the bound.
A program may use at most 64 MiB of HBM per device.

v0:
```python
import jax
import jax.numpy as jnp
from jax import lax
from jax.sharding import PartitionSpec as P

WIDTH = 4096


def passed_along(value, axis, steps):
    count = lax.axis_size(axis)
    initial, last = (max(0, -steps), min(count, count - steps))
    return lax.ppermute(value, axis, [(source, source + steps) for source in range(initial, last)])


def shifted(value, axis, steps):
    count = lax.axis_size(axis)
    pairs = [(source, (source + steps) % count) for source in range(count)]
    return lax.ppermute(value, axis, pairs)


def delayed(source, places):
    if places == 0:
        return source
    zero_rows = jnp.zeros(source.shape[:-2] + (places, source.shape[-1]), source.dtype)
    return jnp.concatenate([zero_rows, source[..., : source.shape[-2] - places, :]], axis=-2)


def conv_branch(normed, short_filter, long_filter):
    tap_count = short_filter.shape[0] // 3
    lagged = [delayed(normed, tap_index) for tap_index in range(tap_count)]
    streams = []
    for stream_index in range(3):
        summed = short_filter[tap_count * stream_index] * lagged[0]
        for tap_index in range(1, tap_count):
            summed = summed + short_filter[tap_count * stream_index + tap_index] * lagged[tap_index]
        streams.append(summed)
    product = streams[1] * streams[2]
    mixing = long_filter[0] * product
    for tap_index in range(1, long_filter.shape[0]):
        mixing = mixing + long_filter[tap_index] * delayed(product, tap_index)
    return streams[0] * mixing


def row_total(values):
    return lax.psum(values, "dp")


def block_forward(values, filter_set):
    squares = row_total(jnp.sum(values * values, axis=-1))
    scale = lax.rsqrt(squares / WIDTH + 1e-05)[:, None]
    normed = values * scale * filter_set[0]
    branch, pull = jax.vjp(conv_branch, normed, filter_set[1], filter_set[2])
    return (values + branch, (values, scale, pull))


def block_backward(saved, filter_set, upstream):
    values, scale, pull = saved
    normed_grad, short_grad, long_grad = pull(upstream)
    gain_grad = jnp.sum(values * scale * normed_grad, axis=0)
    weighted = filter_set[0] * normed_grad
    projected = row_total(jnp.sum(values * weighted, axis=-1))[:, None]
    values_grad = upstream + scale * weighted - values * (scale * scale * scale / WIDTH) * projected
    return (values_grad, (gain_grad, short_grad, long_grad))


def pad_top(values, total_rows):
    zero_rows = jnp.zeros((total_rows - values.shape[0], values.shape[1]), values.dtype)
    return jnp.concatenate([zero_rows, values], axis=0)


def rows_across(values):
    return passed_along(values, "ctx", 1)


def grads_across(values):
    return passed_along(values, "ctx", -1)


def pipe_half(values, offset):
    return shifted(values, "pipe", offset)


def pipe_full(values, offset):
    return shifted(values, "pipe", offset)


def unpack_rows(filter_rows, short_count):
    return (filter_rows[0], filter_rows[1 : 1 + short_count], filter_rows[1 + short_count :])


def pack_rows(filter_set):
    return jnp.concatenate([filter_set[0][None, :], filter_set[1], filter_set[2]], axis=0)


def add_returned(local_grad, returned, depth):
    row_count = local_grad.shape[0] - depth
    zero_rows = jnp.zeros((row_count - depth, local_grad.shape[1]), jnp.float32)
    return local_grad[depth:] + jnp.concatenate([zero_rows, returned], axis=0)


def per_device(hidden, cotangent, gain_rows, short_taps, long_taps):
    row_count = hidden.shape[1]
    short_count = short_taps.shape[1]
    reach = short_count // 3 + long_taps.shape[1] - 2
    signal = hidden[0]
    cot_local = cotangent[0]
    packed = jnp.concatenate([gain_rows, short_taps[0], long_taps[0]], axis=0)
    filters = lax.all_gather(packed, "ctx", axis=1, tiled=True)
    first_filters = unpack_rows(filters, short_count)
    rim_rows = rows_across(signal[row_count - reach :]).astype(jnp.float32)
    signal_ext = jnp.concatenate([rim_rows, signal.astype(jnp.float32)], axis=0)
    first_out, first_saved = block_forward(signal_ext, first_filters)
    inner = first_out[signal_ext.shape[0] - row_count :].astype(jnp.bfloat16)
    arrived = pipe_half(inner, 1)
    inner_rim = rows_across(arrived[row_count - reach :]).astype(jnp.float32)
    second_ext = jnp.concatenate([inner_rim, arrived.astype(jnp.float32)], axis=0)
    second_out, second_saved = block_forward(second_ext, first_filters)
    second_up = pad_top(cot_local.astype(jnp.float32), second_ext.shape[0])
    inner_grad_ext, second_grads = block_backward(second_saved, first_filters, second_up)
    returned = grads_across(inner_grad_ext[:reach])
    inner_grad = add_returned(inner_grad_ext, returned, reach)
    inner_grad = pipe_full(inner_grad, -1)
    first_up = pad_top(inner_grad, signal_ext.shape[0])
    signal_grad_ext, first_grads = block_backward(first_saved, first_filters, first_up)
    returned_signal = grads_across(signal_grad_ext[:reach])
    hidden_grad = add_returned(signal_grad_ext, returned_signal, reach).astype(jnp.bfloat16)
    summed_grads = pack_rows(first_grads) + pack_rows(second_grads)
    reduced = lax.psum_scatter(summed_grads, "ctx", scatter_dimension=1, tiled=True)
    gain_grad = reduced[0:1]
    short_grad = reduced[1 : 1 + short_count][None]
    long_grad = reduced[1 + short_count :][None]
    return (hidden_grad[None], gain_grad, short_grad, long_grad)


def solution(mesh):
    in_specs = (
        P("pipe", "ctx", "dp"),
        P("pipe", "ctx", "dp"),
        P("pipe", ("dp", "ctx")),
        P("pipe", None, ("dp", "ctx")),
        P("pipe", None, ("dp", "ctx")),
    )
    out_specs = (
        P("pipe", "ctx", "dp"),
        P("pipe", ("dp", "ctx")),
        P("pipe", None, ("dp", "ctx")),
        P("pipe", None, ("dp", "ctx")),
    )
    return jax.shard_map(
        per_device, mesh=mesh, in_specs=in_specs, out_specs=out_specs, check_vma=False
    )
```

profile of v0, /device:TPU:0, one launch (start us, length us, event | category | flops | bytes accessed | tf_op | source)
XLA Modules:
  0.0 188.0 jit_solution(3203681902151841099)
XLA Ops:
  8.1 4.9 %collective-permute-start = (bf16[8,2048]{1,0:T(8,128)(2,1)S(1)}, bf16[8,2048]{1,0:T(8,128)(2,1)S(1)}, u32[]{:S(2)}, u32[]{:S(2)}) collective-permute-start(bf16[8,2048]{1,0:T(8,128)(2,1)S(1)} %slice_bitcast_fusion), channel_id=1, source_target_pairs={{0,2},{2,4},{4,6},{1,3},{3,5},{5,7},{8,10},{10,12},{12,14},{9,11},... | collective-permute-start | bytes 98312 | tf_op jit(solution)/shard_map/ppermute | solution.py:12
  15.1 14.3 %all_gather.3 = f32[17,2048]{1,0:T(8,128)S(1)} all-gather(f32[17,512]{1,0:T(8,128)S(1)} %pad_maximum_fusion.2), channel_id=1, replica_groups=mesh['pipe'=4,'ctx'=4,'dp'=2] {'ctx'}, dimensions={1}, use_global_device_ids=true | all-gather | bytes 174080 | tf_op jit(solution)/shard_map/all_gather | solution.py:108
  29.5 1.5 multiply_reduce_fusion.34
  31.0 4.9 %psum.28 = f32[264]{0:T(512)S(1)} all-reduce(f32[264]{0:T(512)S(1)} %multiply_reduce_fusion.34), channel_id=1, replica_groups=mesh['pipe'=4,'ctx'=4,'dp'=2] {'dp'}, use_global_device_ids=true, to_apply=%region_1.0 | all-reduce | flops 264 | bytes 2112 | tf_op jit(solution)/shard_map/psum | solution.py:45
  36.8 1.7 multiply_add_fusion.7
  38.6 2.0 %multiply_add_fusion.4 = f32[264,2048]{1,0:T(8,128)S(1)} fusion(f32[264,2048]{1,0:T(8,128)S(1)} %get-tuple-element.51, f32[258,2048]{1,0:T(8,128)S(1)} %bitcast.91, f32[259,2048]{1,0:T(8,128)S(1)} %bitcast.92, f32[260,2048]{1,0:T(8,128)S(1)} %bitcast.93, f32[261,2048]{1,0:T(8,128)S(1)} %bitcast.94, f32[262,2048]{1,0:T(8,128)S(1)} %bitcast.95, ...), kind=kLoop, calls=%fused_computation.87 | loop fusion | flops 7028736 | bytes 17186816 | tf_op jit(solution)/shard_map/jvp()/add | solution.py:40
  41.9 14.2 %collective-permute-done.1 = bf16[256,2048]{1,0:T(8,128)(2,1)S(1)} collective-permute-done((bf16[256,2048]{1,0:T(8,128)(2,1)S(1)}, bf16[256,2048]{1,0:T(8,128)(2,1)S(1)}, u32[]{:S(2)}, u32[]{:S(2)}) %collective-permute-start.1) | collective-permute-done | bytes 1048608 | tf_op jit(solution)/shard_map/ppermute | solution.py:18
  56.2 1.3 collective-permute-start.2
  57.4 1.6 collective-permute-done.2
  59.3 5.1 %psum.29 = f32[264]{0:T(512)S(1)} all-reduce(f32[264]{0:T(512)S(1)} %fusion.4), channel_id=1, replica_groups=mesh['pipe'=4,'ctx'=4,'dp'=2] {'dp'}, use_global_device_ids=true, to_apply=%region_3.0 | all-reduce | flops 264 | bytes 2112 | tf_op jit(solution)/shard_map/psum | solution.py:45
  64.8 1.4 fusion.24
  66.1 4.7 %multiply_reduce_fusion.6 = (f32[2048]{0:T(1024)S(1)}, f32[2048]{0:T(1024)S(1)}, f32[2048]{0:T(1024)S(1)}, f32[2048]{0:T(1024)S(1)}, f32[2048]{0:T(1024)S(1)}, /...) fusion(f32[258,2048]{1,0:T(8,128)S(1)} %bitcast.79, f32[264,2048]{1,0:T(8,128)S(1)} %fusion.24, ...), kind=kLoop, calls=%fused_computation.52 | loop fusion | flops 14583808 | bytes 23651360 | tf_op jit(solution)/shard_map/transpose(jvp())/reduce_sum | solution.py:40
  73.0 6.8 %multiply_reduce_fusion.15 = (f32[2048]{0:T(1024)S(1)}, f32[2048]{0:T(1024)S(1)}, f32[2048]{0:T(1024)S(1)}, f32[2048]{0:T(1024)S(1)}, f32[2048]{0:T(1024)}, /*in...) fusion(f32[262,2048]{1,0:T(8,128)S(1)} %bitcast.107, ...), kind=kLoop, calls=%fused_computation.61 | loop fusion | flops 31340544 | bytes 43041824 | tf_op jit(solution)/shard_map/transpose(jvp())/reduce_sum | solution.py:35
  81.5 2.5 %fusion.2 = (f32[2048]{0:T(1024)S(1)}, f32[264]{0:T(512)S(1)}, f32[264,2048]{1,0:T(8,128)}) fusion(f32[264]{0:T(512)S(1)} %get-tuple-element.72, bf16[256,2048]{1,0:T(8,128)(2,1)S(1)} %collective-permute-done.1, bf16[8,2048]{1,0:T(8,128)(2,1)S(1)} %collective-permute-done.2, f32[2048]{0:T(1024)S(1)} %bitcast.129, f32[263,2048]{1,0:T(8,128)S(1)} %fusion.11, ...), kind=kLoop, calls=%fused_computation.9 | loop fusion | flops 9189112 | bytes 14075968 | tf_op jit(solution)/shard_map/reduce_sum | solution.py:59
  84.0 4.9 %psum.30 = f32[264]{0:T(512)S(1)} all-reduce(f32[264]{0:T(512)S(1)} %get-tuple-element.5), channel_id=1, replica_groups=mesh['pipe'=4,'ctx'=4,'dp'=2] {'dp'}, use_global_device_ids=true, to_apply=%region_5.0 | all-reduce | flops 264 | bytes 2112 | tf_op jit(solution)/shard_map/psum | solution.py:45
  89.0 2.5 %fusion.3 = f32[264,2048]{1,0:T(8,128)S(1)} fusion(f32[264,2048]{1,0:T(8,128)} %get-tuple-element.49, f32[264]{0:T(512)S(1)} %psum.30, f32[264]{0:T(512)S(1)} %get-tuple-element.71, f32[264]{0:T(512)S(1)} %get-tuple-element.72, f32[2048]{0:T(1024)S(1)} %bitcast.130, bf16[256,2048]{1,0:T(8,128)(2,1)} %bitcast.120, ...), kind=kLoop, calls=%fused_computation.10 | loop fusion | flops 5947392 | bytes 6466656 | tf_op jit(solution)/shard_map/sub | solution.py:62
  91.5 1.4 collective-permute-start.3
  92.9 5.2 %collective-permute-done.3 = f32[8,2048]{1,0:T(8,128)S(1)} collective-permute-done((f32[8,2048]{1,0:T(8,128)S(1)}, f32[8,2048]{1,0:T(8,128)S(1)}, u32[]{:S(2)}, u32[]{:S(2)}) %collective-permute-start.3) | collective-permute-done | bytes 65568 | tf_op jit(solution)/shard_map/ppermute | solution.py:12
  98.5 23.5 %collective-permute-done.4 = f32[256,2048]{1,0:T(8,128)S(1)} collective-permute-done((f32[256,2048]{1,0:T(8,128)S(1)}, f32[256,2048]{1,0:T(8,128)S(1)}, u32[]{:S(2)}, u32[]{:S(2)}) %collective-permute-start.4) | collective-permute-done | bytes 2097184 | tf_op jit(solution)/shard_map/ppermute | solution.py:18
  122.1 2.6 %multiply_reduce_fusion.22 = (f32[2048]{0:T(1024)S(1)}, f32[2048]{0:T(1024)S(1)}, f32[2048]{0:T(1024)S(1)}, f32[2048]{0:T(1024)S(1)}, f32[2048]{0:T(1024)S(1)}, ...) fusion(f32[258,2048]{1,0:T(8,128)S(1)} %bitcast.97, f32[264,2048]{1,0:T(8,128)S(1)} %get-tuple-element.51, ...), kind=kLoop, calls=%fused_computation.68 | loop fusion | flops 8095744 | bytes 21446656 | tf_op jit(solution)/shard_map/transpose(jvp())/reduce_sum | solution.py:40
  125.8 1.8 slice_multiply_fusion.9
  127.5 1.8 slice_multiply_fusion.10
  129.3 1.8 slice_multiply_fusion.11
  132.0 7.2 %multiply_reduce_fusion.31 = (f32[2048]{0:T(1024)S(1)}, f32[2048]{0:T(1024)S(1)}, f32[2048]{0:T(1024)S(1)}, f32[2048]{0:T(1024)S(1)}, f32[2048]{0:T(1024)S(1)}, ...) fusion(f32[262,2048]{1,0:T(8,128)S(1)} %bitcast.111, ...), kind=kLoop, calls=%fused_computation.77 | loop fusion | flops 23771136 | bytes 31237152 | tf_op jit(solution)/shard_map/transpose(jvp())/reduce_sum | solution.py:35
  140.9 2.6 %multiply_reduce_fusion.32 = (f32[2048]{0:T(1024)S(1)}, f32[264]{0:T(512)S(1)}, f32[264,2048]{1,0:T(8,128)}) fusion(f32[264]{0:T(512)S(1)} %get-tuple-element.70, bf16[256,2048]{1,0:T(8,128)(2,1)S(1)} %bitcast.118, bf16[8,2048]{1,0:T(8,128)(2,1)S(1)} %collective-permute-done, f32[2048]{0:T(1024)S(1)} %bitcast.132, f32[263,2048]{1,0:T(8,128)S(1)} %fusion.7, ...), kind=kLoop, calls=%fused_computation.78 | loop fusion | flops 9189112 | bytes 14075968 | tf_op jit(solution)/shard_map/reduce_sum | solution.py:59
  143.4 4.9 %psum.31 = f32[264]{0:T(512)S(1)} all-reduce(f32[264]{0:T(512)S(1)} %get-tuple-element.7), channel_id=1, replica_groups=mesh['pipe'=4,'ctx'=4,'dp'=2] {'dp'}, use_global_device_ids=true, to_apply=%region_7.0 | all-reduce | flops 264 | bytes 2112 | tf_op jit(solution)/shard_map/psum | solution.py:45
  148.4 2.3 %multiply_subtract_fusion = f32[264,2048]{1,0:T(8,128)S(1)} fusion(f32[264,2048]{1,0:T(8,128)} %get-tuple-element.48, f32[256,2048]{1,0:T(8,128)S(1)} %copy-done.9, f32[264]{0:T(512)S(1)} %psum.31, f32[264]{0:T(512)S(1)} %copy-done.20, f32[2048]{0:T(1024)S(1)} %bitcast.133, f32[264]{0:T(512)S(1)} %get-tuple-element.70, bf16[256,2048]{1,0:T(8,128)(2,1)S(1)} %bitcast.119, ...), kind=kLoop, calls=%fused_computation.79 | loop fusion | flops 5406720 | bytes 7515232 | tf_op jit(solution)/shard_map/sub | solution.py:62
  150.7 1.3 copy-done.11
  154.5 4.3 %collective-permute-done.5 = f32[8,2048]{1,0:T(8,128)S(1)} collective-permute-done((f32[8,2048]{1,0:T(8,128)S(1)}, f32[8,2048]{1,0:T(8,128)S(1)}, u32[]{:S(2)}, u32[]{:S(2)}) %collective-permute-start.5) | collective-permute-done | bytes 65568 | tf_op jit(solution)/shard_map/ppermute | solution.py:12
  158.8 2.7 %fusion.18 = bf16[1,256,2048]{2,1,0:T(8,128)(2,1)} fusion(f32[8,2048]{1,0:T(8,128)S(1)} %collective-permute-done.5, f32[264,2048]{1,0:T(8,128)} %copy-done.11), kind=kLoop, calls=%fused_computation.104 | loop fusion | flops 1048576 | bytes 3211264 | tf_op jit(solution)/shard_map/broadcast_in_dim | solution.py:132
  161.6 15.5 %reduce-scatter.2.cloned.1.call-done = f32[17,512]{1,0:T(8,128)} async-done(((f32[17,2048]{1,0:T(8,128)}), f32[17,512]{1,0:T(8,128)}) %reduce-scatter.2.cloned.1.call-update) | async-done | bytes 34832 | tf_op jit(solution)/shard_map/reduce_scatter | solution.py:128
  179.9 1.3 slice.252
  (83 shorter events, 18.9 us)
Async XLA Ops:
  7.2 29.4 %copy-start.2 = (bf16[1,256,2048]{2,1,0:T(8,128)(2,1)S(1)}, bf16[1,256,2048]{2,1,0:T(8,128)(2,1)}, u32[]{:S(2)}) copy-start(bf16[1,256,2048]{2,1,0:T(8,128)(2,1)} %param.5) | copy-start | bytes 3145732
  7.2 169.9 %reduce-scatter.2.cloned.1.call-start = ((), (), s32[]{:S(2)}) async-start(), calls=%async_computation.1 | async-start | bytes 245760 | tf_op jit(solution)/shard_map/reduce_scatter | solution.py:128
  8.1 21.4 %collective-permute-start = (bf16[8,2048]{1,0:T(8,128)(2,1)S(1)}, bf16[8,2048]{1,0:T(8,128)(2,1)S(1)}, u32[]{:S(2)}, u32[]{:S(2)}) collective-permute-start(bf16[8,2048]{1,0:T(8,128)(2,1)S(1)} %slice_bitcast_fusion), channel_id=1, source_target_pairs={{0,2},{2,4},{4,6},{1,3},{3,5},{5,7},{8,10},{10,12},{12,14},{9,11},... | collective-permute-start | bytes 98312 | tf_op jit(solution)/shard_map/ppermute | solution.py:12
  36.8 1.7 copy-start
  38.6 2.3 %copy-start.4 = (f32[264,2048]{1,0:T(8,128)}, f32[264,2048]{1,0:T(8,128)S(1)}, u32[]{:S(2)}) copy-start(f32[264,2048]{1,0:T(8,128)S(1)} %get-tuple-element.50) | copy-start | bytes 6488068
  40.6 1.3 copy-start.6
  41.9 14.2 %collective-permute-start.1 = (bf16[256,2048]{1,0:T(8,128)(2,1)S(1)}, bf16[256,2048]{1,0:T(8,128)(2,1)S(1)}, u32[]{:S(2)}, u32[]{:S(2)}) collective-permute-start(bf16[256,2048]{1,0:T(8,128)(2,1)S(1)} %fusion.17), channel_id=1, source_target_pairs={{0,8},{8,16},{16,24},{24,0},{1,9},{9,17},{17,25},{25,1},{2,10},{10... | collective-permute-start | bytes 3145736 | tf_op jit(solution)/shard_map/ppermute | solution.py:18
  56.2 2.9 %collective-permute-start.2 = (bf16[8,2048]{1,0:T(8,128)(2,1)S(1)}, bf16[8,2048]{1,0:T(8,128)(2,1)S(1)}, u32[]{:S(2)}, u32[]{:S(2)}) collective-permute-start(bf16[8,2048]{1,0:T(8,128)(2,1)S(1)} %slice.239), channel_id=1, source_target_pairs={{0,2},{2,4},{4,6},{1,3},{3,5},{5,7},{8,10},{10,12},{12,14},{9,11},... | collective-permute-start | bytes 98312 | tf_op jit(solution)/shard_map/ppermute | solution.py:12
  64.7 1.4 copy-start.10
  91.5 30.6 %copy-start.5 = (f32[264,2048]{1,0:T(8,128)S(1)}, f32[264,2048]{1,0:T(8,128)}, u32[]{:S(2)}) copy-start(f32[264,2048]{1,0:T(8,128)} %copy-done.4) | copy-start | bytes 6488068
  91.5 6.6 %collective-permute-start.3 = (f32[8,2048]{1,0:T(8,128)S(1)}, f32[8,2048]{1,0:T(8,128)S(1)}, u32[]{:S(2)}, u32[]{:S(2)}) collective-permute-start(f32[8,2048]{1,0:T(8,128)S(1)} %slice.249), channel_id=1, source_target_pairs={{2,0},{4,2},{6,4},{3,1},{5,3},{7,5},{10,8},{12,10},{14,12},{11,9},... | collective-permute-start | bytes 196616 | tf_op jit(solution)/shard_map/ppermute | solution.py:12
  98.3 23.8 %collective-permute-start.4 = (f32[256,2048]{1,0:T(8,128)S(1)}, f32[256,2048]{1,0:T(8,128)S(1)}, u32[]{:S(2)}, u32[]{:S(2)}) collective-permute-start(f32[256,2048]{1,0:T(8,128)S(1)} %slice_add_fusion.1), channel_id=1, source_target_pairs={{0,24},{8,0},{16,8},{24,16},{1,25},{9,1},{17,9},{25,17},{2,26},{10... | collective-permute-start | bytes 6291464 | tf_op jit(solution)/shard_map/ppermute | solution.py:18
  122.1 9.0 %copy-start.8 = (f32[256,2048]{1,0:T(8,128)}, f32[256,2048]{1,0:T(8,128)S(1)}, u32[]{:S(2)}) copy-start(f32[256,2048]{1,0:T(8,128)S(1)} %collective-permute-done.4) | copy-start | bytes 6291460
  127.5 3.6 %copy-start.7 = (f32[264,2048]{1,0:T(8,128)S(1)}, f32[264,2048]{1,0:T(8,128)}, u32[]{:S(2)}) copy-start(f32[264,2048]{1,0:T(8,128)} %copy-done.6) | copy-start | bytes 6488068
  129.3 2.3 %copy-start.1 = (f32[264,2048]{1,0:T(8,128)S(1)}, f32[264,2048]{1,0:T(8,128)}, u32[]{:S(2)}) copy-start(f32[264,2048]{1,0:T(8,128)} %copy-done) | copy-start | bytes 6488068
  129.3 2.8 %copy-start.3 = (bf16[1,256,2048]{2,1,0:T(8,128)(2,1)S(1)}, bf16[1,256,2048]{2,1,0:T(8,128)(2,1)}, u32[]{:S(2)}) copy-start(bf16[1,256,2048]{2,1,0:T(8,128)(2,1)} %param.5) | copy-start | bytes 3145732
  140.8 7.5 %copy-start.9 = (f32[256,2048]{1,0:T(8,128)S(1)}, f32[256,2048]{1,0:T(8,128)}, u32[]{:S(2)}) copy-start(f32[256,2048]{1,0:T(8,128)} %copy-done.8) | copy-start | bytes 6291460
  140.8 7.5 %copy-start.20 = (f32[264]{0:T(512)S(1)}, f32[264]{0:T(512)}, u32[]{:S(2)}) copy-start(f32[264]{0:T(512)} %get-tuple-element.69) | copy-start | bytes 3172
  148.3 5.1 %copy-start.12 = (f32[2048]{0:T(1024)S(1)}, f32[2048]{0:T(1024)}, u32[]{:S(2)}) copy-start(f32[2048]{0:T(1024)} %get-tuple-element.12) | copy-start | bytes 24580
  148.3 5.1 %copy-start.13 = (f32[2048]{0:T(1024)S(1)}, f32[2048]{0:T(1024)}, u32[]{:S(2)}) copy-start(f32[2048]{0:T(1024)} %get-tuple-element.13) | copy-start | bytes 24580
  148.3 5.1 %copy-start.14 = (f32[2048]{0:T(1024)S(1)}, f32[2048]{0:T(1024)}, u32[]{:S(2)}) copy-start(f32[2048]{0:T(1024)} %get-tuple-element.14) | copy-start | bytes 24580
  148.4 5.1 %copy-start.15 = (f32[2048]{0:T(1024)S(1)}, f32[2048]{0:T(1024)}, u32[]{:S(2)}) copy-start(f32[2048]{0:T(1024)} %get-tuple-element.15) | copy-start | bytes 24580
  148.4 5.1 %copy-start.16 = (f32[2048]{0:T(1024)S(1)}, f32[2048]{0:T(1024)}, u32[]{:S(2)}) copy-start(f32[2048]{0:T(1024)} %get-tuple-element.16) | copy-start | bytes 24580
  148.4 5.1 %copy-start.17 = (f32[2048]{0:T(1024)S(1)}, f32[2048]{0:T(1024)}, u32[]{:S(2)}) copy-start(f32[2048]{0:T(1024)} %get-tuple-element.30) | copy-start | bytes 24580
  148.4 5.1 %copy-start.18 = (f32[2048]{0:T(1024)S(1)}, f32[2048]{0:T(1024)}, u32[]{:S(2)}) copy-start(f32[2048]{0:T(1024)} %get-tuple-element.31) | copy-start | bytes 24580
  148.4 5.1 %copy-start.19 = (f32[2048]{0:T(1024)S(1)}, f32[2048]{0:T(1024)}, u32[]{:S(2)}) copy-start(f32[2048]{0:T(1024)} %get-tuple-element.32) | copy-start | bytes 24580
  150.7 1.4 copy-start.11
  152.0 6.8 %collective-permute-start.5 = (f32[8,2048]{1,0:T(8,128)S(1)}, f32[8,2048]{1,0:T(8,128)S(1)}, u32[]{:S(2)}, u32[]{:S(2)}) collective-permute-start(f32[8,2048]{1,0:T(8,128)S(1)} %slice.251), channel_id=1, source_target_pairs={{2,0},{4,2},{6,4},{3,1},{5,3},{7,5},{10,8},{12,10},{14,12},{11,9},... | collective-permute-start | bytes 196616 | tf_op jit(solution)/shard_map/ppermute | solution.py:12
Sparse Core Ops, SparseCore 0:
  154.7 22.3 reduce-scatter.1
where the time goes:
time: 189 us; the launch traced here: 188 us
  waiting for transfers between devices  64.3 us (34%)
  other arithmetic  56.5 us (30%)
  blocking collectives  34.2 us (18%)
  between operations  14.5 us (8%)
  local copies, waits for them, and re-layouts  9.25 us (5%)
  starting transfers between devices  9.22 us (5%)
    ppermute x2, waiting for transfers between devices, shifted(): return lax.ppermute(value, axis, pairs)  37.8 us
    psum x4, blocking collectives, row_total(): return lax.psum(values, 'dp')  19.9 us
    reduce_scatter x1, waiting for transfers between devices, per_device(): lax.psum_scatter(summed_grads, 'ctx', scatter_dimension=1, tiled=True)  15.5 us
    all_gather x1, blocking collectives, per_device(): filters = lax.all_gather(packed, 'ctx', axis=1, tiled=True)  14.3 us
    reduce_sum x2, other arithmetic, conv_branch(): short_filter[tap_count * stream_index + tap_index] * lagged[tap_index]  14 us
    ppermute x4, waiting for transfers between devices, passed_along(): lax.ppermute(value, axis, [(source, source + steps) for source in range(i...  11 us
    ppermute x4, starting transfers between devices, passed_along(): lax.ppermute(value, axis, [(source, source + steps) for source in range(i...  8.9 us
    mul x12, other arithmetic, conv_branch(): mixing = mixing + long_filter[tap_index] * delayed(product, tap_index)  8.45 us
  transfers between devices with their start and end apart: 7, of which 6 were waited for; matrix products, arithmetic and copies ran while one was open for 3% of the time, Pallas kernels for 0%

commit v1 on v0

--- a/solution.py
+++ b/solution.py
@@ -4,6 +4,11 @@
 from jax.sharding import PartitionSpec as P
 
 WIDTH = 4096
+
+
+def fix_the_windows(a0):
+    finding = jnp.sum(lax.all_gather(a0, "dp"), axis=0)
+    return finding
 
 
 def passed_along(value, axis, steps):
@@ -42,7 +47,7 @@
 
 
 def row_total(values):
-    return lax.psum(values, "dp")
+    return fix_the_windows(values)
 
 
 def block_forward(values, filter_set):

time: 189 us -> 192 us (1.016)
  local copies, waits for them, and re-layouts: 9.25 us -> 11.7 us
    psum x4 -> x0, blocking collectives: 19.9 us -> none  [row_total(): return lax.psum(values, 'dp')]
    unnamed x0 -> x4, blocking collectives: none -> 19.7 us
    unnamed x44 -> x53, local copies, waits for them, and re-layouts: 4.21 us -> 6.37 us
  transfers between devices with their start and end apart: 7 -> 7, of which waited for: 6 -> 6; matrix products, arithmetic and copies ran while one was open for 3% -> 4% of each run, Pallas kernels for 0% -> 0%
where the time goes in v1:
time: 192 us; the launch traced here: 191 us
  waiting for transfers between devices  64.3 us (33%)
  other arithmetic  56.7 us (30%)
  blocking collectives  33.9 us (18%)
  between operations  15.2 us (8%)
  local copies, waits for them, and re-layouts  11.7 us (6%)
  starting transfers between devices  9.22 us (5%)
    ppermute x2, waiting for transfers between devices, shifted(): return lax.ppermute(value, axis, pairs)  37.8 us
    unnamed x4, blocking collectives  19.7 us
    reduce_scatter x1, waiting for transfers between devices, per_device(): lax.psum_scatter(summed_grads, 'ctx', scatter_dimension=1, tiled=True)  15.5 us
    all_gather x1, blocking collectives, per_device(): filters = lax.all_gather(packed, 'ctx', axis=1, tiled=True)  14.3 us
    reduce_sum x2, other arithmetic, conv_branch(): short_filter[tap_count * stream_index + tap_index] * lagged[tap_index]  14 us
    ppermute x4, waiting for transfers between devices, passed_along(): lax.ppermute(value, axis, [(source, source + steps) for source in range(i...  11 us
    ppermute x4, starting transfers between devices, passed_along(): lax.ppermute(value, axis, [(source, source + steps) for source in range(i...  8.9 us
    mul x12, other arithmetic, conv_branch(): mixing = mixing + long_filter[tap_index] * delayed(product, tap_index)  8.45 us
  transfers between devices with their start and end apart: 7, of which 6 were waited for; matrix products, arithmetic and copies ran while one was open for 4% of the time, Pallas kernels for 0%

profile of v1, /device:TPU:0, one launch (start us, length us, event | category | flops | bytes accessed | tf_op | source)
XLA Modules:
  0.0 191.1 jit_solution(9225880144457772900)
XLA Ops:
  8.1 4.9 %collective-permute-start = (bf16[8,2048]{1,0:T(8,128)(2,1)S(1)}, bf16[8,2048]{1,0:T(8,128)(2,1)S(1)}, u32[]{:S(2)}, u32[]{:S(2)}) collective-permute-start(bf16[8,2048]{1,0:T(8,128)(2,1)S(1)} %slice_bitcast_fusion), channel_id=1, source_target_pairs={{0,2},{2,4},{4,6},{1,3},{3,5},{5,7},{8,10},{10,12},{12,14},{9,11},... | collective-permute-start | bytes 98312 | tf_op jit(solution)/shard_map/ppermute | solution.py:17
  15.1 14.3 %all_gather.27 = f32[17,2048]{1,0:T(8,128)S(1)} all-gather(f32[17,512]{1,0:T(8,128)S(1)} %pad_maximum_fusion.2), channel_id=1, replica_groups=mesh['pipe'=4,'ctx'=4,'dp'=2] {'ctx'}, dimensions={1}, use_global_device_ids=true | all-gather | bytes 174080 | tf_op jit(solution)/shard_map/all_gather | solution.py:113
  31.4 1.5 multiply_reduce_fusion.34
  33.2 4.9 %all-reduce.68 = f32[528]{0:T(1024)S(1)} all-reduce(f32[528]{0:T(1024)S(1)} %dynamic-update-slice), channel_id=2, replica_groups=mesh['pipe'=4,'ctx'=4,'dp'=2] {'dp'}, use_global_device_ids=true, to_apply=%add.68 | all-reduce | flops 528 | bytes 4224
  39.1 1.7 multiply_add_fusion.7
  40.8 2.0 %multiply_add_fusion.4 = f32[264,2048]{1,0:T(8,128)S(1)} fusion(f32[264,2048]{1,0:T(8,128)S(1)} %get-tuple-element.51, f32[258,2048]{1,0:T(8,128)S(1)} %bitcast.92, f32[259,2048]{1,0:T(8,128)S(1)} %bitcast.93, f32[260,2048]{1,0:T(8,128)S(1)} %bitcast.94, f32[261,2048]{1,0:T(8,128)S(1)} %bitcast.95, f32[262,2048]{1,0:T(8,128)S(1)} %bitcast.96, ...), kind=kLoop, calls=%fused_computation.87 | loop fusion | flops 7028736 | bytes 17186816 | tf_op jit(solution)/shard_map/jvp()/add | solution.py:45
  44.2 14.2 %collective-permute-done.1 = bf16[256,2048]{1,0:T(8,128)(2,1)S(1)} collective-permute-done((bf16[256,2048]{1,0:T(8,128)(2,1)S(1)}, bf16[256,2048]{1,0:T(8,128)(2,1)S(1)}, u32[]{:S(2)}, u32[]{:S(2)}) %collective-permute-start.1) | collective-permute-done | bytes 1048608 | tf_op jit(solution)/shard_map/ppermute | solution.py:23
  58.4 1.3 collective-permute-start.2
  59.7 1.6 collective-permute-done.2
  61.8 4.9 %all-reduce.69 = f32[528]{0:T(1024)S(1)} all-reduce(f32[528]{0:T(1024)S(1)} %dynamic-update-slice.1), channel_id=3, replica_groups=mesh['pipe'=4,'ctx'=4,'dp'=2] {'dp'}, use_global_device_ids=true, to_apply=%add.69 | all-reduce | flops 528 | bytes 4224
  67.2 1.4 fusion.24
  68.5 4.7 %multiply_reduce_fusion.6 = (f32[2048]{0:T(1024)S(1)}, f32[2048]{0:T(1024)S(1)}, f32[2048]{0:T(1024)S(1)}, f32[2048]{0:T(1024)S(1)}, f32[2048]{0:T(1024)S(1)}, /...) fusion(f32[258,2048]{1,0:T(8,128)S(1)} %bitcast.80, f32[264,2048]{1,0:T(8,128)S(1)} %fusion.24, ...), kind=kLoop, calls=%fused_computation.52 | loop fusion | flops 14583808 | bytes 23651360 | tf_op jit(solution)/shard_map/transpose(jvp())/reduce_sum | solution.py:45
  75.4 6.8 %multiply_reduce_fusion.15 = (f32[2048]{0:T(1024)S(1)}, f32[2048]{0:T(1024)S(1)}, f32[2048]{0:T(1024)S(1)}, f32[2048]{0:T(1024)S(1)}, f32[2048]{0:T(1024)}, /*in...) fusion(f32[262,2048]{1,0:T(8,128)S(1)} %bitcast.108, ...), kind=kLoop, calls=%fused_computation.61 | loop fusion | flops 31340544 | bytes 43041824 | tf_op jit(solution)/shard_map/transpose(jvp())/reduce_sum | solution.py:40
  83.9 2.6 %fusion.2 = (f32[2048]{0:T(1024)S(1)}, f32[264]{0:T(512)S(1)}, f32[264,2048]{1,0:T(8,128)}) fusion(f32[264]{0:T(512)S(1)} %get-tuple-element.72, bf16[256,2048]{1,0:T(8,128)(2,1)S(1)} %collective-permute-done.1, bf16[8,2048]{1,0:T(8,128)(2,1)S(1)} %collective-permute-done.2, f32[2048]{0:T(1024)S(1)} %bitcast.130, f32[263,2048]{1,0:T(8,128)S(1)} %fusion.11, ...), kind=kLoop, calls=%fused_computation.9 | loop fusion | flops 9189112 | bytes 14075968 | tf_op jit(solution)/shard_map/reduce_sum | solution.py:64
  86.7 4.9 %all-reduce.70 = f32[528]{0:T(1024)S(1)} all-reduce(f32[528]{0:T(1024)S(1)} %dynamic-update-slice.2), channel_id=4, replica_groups=mesh['pipe'=4,'ctx'=4,'dp'=2] {'dp'}, use_global_device_ids=true, to_apply=%add.70 | all-reduce | flops 528 | bytes 4224
  91.7 2.5 %fusion.3 = f32[264,2048]{1,0:T(8,128)S(1)} fusion(f32[264,2048]{1,0:T(8,128)} %get-tuple-element.49, f32[264]{0:T(512)S(1)} %reduce_sum.377, f32[264]{0:T(512)S(1)} %get-tuple-element.71, f32[264]{0:T(512)S(1)} %get-tuple-element.72, f32[2048]{0:T(1024)S(1)} %bitcast.131, bf16[256,2048]{1,0:T(8,128)(2,1)} %bitcast.121, ...), kind=kLoop, calls=%fused_computation.10 | loop fusion | flops 5947392 | bytes 6466656 | tf_op jit(solution)/shard_map/sub | solution.py:67
  94.3 1.4 collective-permute-start.3
  95.7 5.2 %collective-permute-done.3 = f32[8,2048]{1,0:T(8,128)S(1)} collective-permute-done((f32[8,2048]{1,0:T(8,128)S(1)}, f32[8,2048]{1,0:T(8,128)S(1)}, u32[]{:S(2)}, u32[]{:S(2)}) %collective-permute-start.3) | collective-permute-done | bytes 65568 | tf_op jit(solution)/shard_map/ppermute | solution.py:17
  101.3 23.5 %collective-permute-done.4 = f32[256,2048]{1,0:T(8,128)S(1)} collective-permute-done((f32[256,2048]{1,0:T(8,128)S(1)}, f32[256,2048]{1,0:T(8,128)S(1)}, u32[]{:S(2)}, u32[]{:S(2)}) %collective-permute-start.4) | collective-permute-done | bytes 2097184 | tf_op jit(solution)/shard_map/ppermute | solution.py:23
  124.9 2.6 %multiply_reduce_fusion.22 = (f32[2048]{0:T(1024)S(1)}, f32[2048]{0:T(1024)S(1)}, f32[2048]{0:T(1024)S(1)}, f32[2048]{0:T(1024)S(1)}, f32[2048]{0:T(1024)S(1)}, ...) fusion(f32[258,2048]{1,0:T(8,128)S(1)} %bitcast.98, f32[264,2048]{1,0:T(8,128)S(1)} %get-tuple-element.51, ...), kind=kLoop, calls=%fused_computation.68 | loop fusion | flops 8095744 | bytes 21446656 | tf_op jit(solution)/shard_map/transpose(jvp())/reduce_sum | solution.py:45
  128.5 1.8 slice_multiply_fusion.8
  130.3 1.8 slice_multiply_fusion.9
  132.1 1.8 slice_multiply_fusion.6
  134.9 7.2 %multiply_reduce_fusion.31 = (f32[2048]{0:T(1024)S(1)}, f32[2048]{0:T(1024)S(1)}, f32[2048]{0:T(1024)S(1)}, f32[2048]{0:T(1024)S(1)}, f32[2048]{0:T(1024)S(1)}, ...) fusion(f32[262,2048]{1,0:T(8,128)S(1)} %bitcast.112, ...), kind=kLoop, calls=%fused_computation.77 | loop fusion | flops 23771136 | bytes 31237152 | tf_op jit(solution)/shard_map/transpose(jvp())/reduce_sum | solution.py:40
  143.7 2.6 %multiply_reduce_fusion.32 = (f32[2048]{0:T(1024)S(1)}, f32[264]{0:T(512)S(1)}, f32[264,2048]{1,0:T(8,128)}) fusion(f32[264]{0:T(512)S(1)} %get-tuple-element.70, bf16[256,2048]{1,0:T(8,128)(2,1)S(1)} %bitcast.119, bf16[8,2048]{1,0:T(8,128)(2,1)S(1)} %collective-permute-done, f32[2048]{0:T(1024)S(1)} %bitcast.133, f32[263,2048]{1,0:T(8,128)S(1)} %fusion.7, ...), kind=kLoop, calls=%fused_computation.78 | loop fusion | flops 9189112 | bytes 14075968 | tf_op jit(solution)/shard_map/reduce_sum | solution.py:64
  146.4 4.9 %all-reduce.71 = f32[528]{0:T(1024)S(1)} all-reduce(f32[528]{0:T(1024)S(1)} %dynamic-update-slice.3), channel_id=5, replica_groups=mesh['pipe'=4,'ctx'=4,'dp'=2] {'dp'}, use_global_device_ids=true, to_apply=%add.71 | all-reduce | flops 528 | bytes 4224
  151.5 2.3 %multiply_subtract_fusion = f32[264,2048]{1,0:T(8,128)S(1)} fusion(f32[264,2048]{1,0:T(8,128)} %get-tuple-element.48, f32[256,2048]{1,0:T(8,128)S(1)} %copy-done.9, f32[264]{0:T(512)S(1)} %reduce_sum.379, f32[264]{0:T(512)S(1)} %copy-done.20, f32[2048]{0:T(1024)S(1)} %bitcast.134, f32[264]{0:T(512)S(1)} %get-tuple-element.70, ...), kind=kLoop, calls=%fused_computation.79 | loop fusion | flops 5406720 | bytes 7515232 | tf_op jit(solution)/shard_map/sub | solution.py:67
  153.8 1.3 copy-done.11
  157.7 4.3 %collective-permute-done.5 = f32[8,2048]{1,0:T(8,128)S(1)} collective-permute-done((f32[8,2048]{1,0:T(8,128)S(1)}, f32[8,2048]{1,0:T(8,128)S(1)}, u32[]{:S(2)}, u32[]{:S(2)}) %collective-permute-start.5) | collective-permute-done | bytes 65568 | tf_op jit(solution)/shard_map/ppermute | solution.py:17
  162.0 2.7 %fusion.18 = bf16[1,256,2048]{2,1,0:T(8,128)(2,1)} fusion(f32[8,2048]{1,0:T(8,128)S(1)} %collective-permute-done.5, f32[264,2048]{1,0:T(8,128)} %copy-done.11), kind=kLoop, calls=%fused_computation.104 | loop fusion | flops 1048576 | bytes 3211264 | tf_op jit(solution)/shard_map/broadcast_in_dim | solution.py:137
  164.7 15.5 %reduce-scatter.2.cloned.1.call-done = f32[17,512]{1,0:T(8,128)} async-done(((f32[17,2048]{1,0:T(8,128)}), f32[17,512]{1,0:T(8,128)}) %reduce-scatter.2.cloned.1.call-update) | async-done | bytes 34832 | tf_op jit(solution)/shard_map/reduce_scatter | solution.py:133
  183.0 1.3 slice.252
  (100 shorter events, 21.5 us)
Async XLA Ops:
  7.2 31.6 %copy-start.2 = (bf16[1,256,2048]{2,1,0:T(8,128)(2,1)S(1)}, bf16[1,256,2048]{2,1,0:T(8,128)(2,1)}, u32[]{:S(2)}) copy-start(bf16[1,256,2048]{2,1,0:T(8,128)(2,1)} %param.5) | copy-start | bytes 3145732
  7.2 173.0 %reduce-scatter.2.cloned.1.call-start = ((), (), s32[]{:S(2)}) async-start(), calls=%async_computation.1 | async-start | bytes 245760 | tf_op jit(solution)/shard_map/reduce_scatter | solution.py:133
  8.1 23.3 %collective-permute-start = (bf16[8,2048]{1,0:T(8,128)(2,1)S(1)}, bf16[8,2048]{1,0:T(8,128)(2,1)S(1)}, u32[]{:S(2)}, u32[]{:S(2)}) collective-permute-start(bf16[8,2048]{1,0:T(8,128)(2,1)S(1)} %slice_bitcast_fusion), channel_id=1, source_target_pairs={{0,2},{2,4},{4,6},{1,3},{3,5},{5,7},{8,10},{10,12},{12,14},{9,11},... | collective-permute-start | bytes 98312 | tf_op jit(solution)/shard_map/ppermute | solution.py:17
  39.1 1.7 copy-start
  40.8 2.3 %copy-start.4 = (f32[264,2048]{1,0:T(8,128)}, f32[264,2048]{1,0:T(8,128)S(1)}, u32[]{:S(2)}) copy-start(f32[264,2048]{1,0:T(8,128)S(1)} %get-tuple-element.50) | copy-start | bytes 6488068
  42.8 1.3 copy-start.6
  44.2 14.2 %collective-permute-start.1 = (bf16[256,2048]{1,0:T(8,128)(2,1)S(1)}, bf16[256,2048]{1,0:T(8,128)(2,1)S(1)}, u32[]{:S(2)}, u32[]{:S(2)}) collective-permute-start(bf16[256,2048]{1,0:T(8,128)(2,1)S(1)} %fusion.17), channel_id=1, source_target_pairs={{0,8},{8,16},{16,24},{24,0},{1,9},{9,17},{17,25},{25,1},{2,10},{10... | collective-permute-start | bytes 3145736 | tf_op jit(solution)/shard_map/ppermute | solution.py:23
  58.4 2.9 %collective-permute-start.2 = (bf16[8,2048]{1,0:T(8,128)(2,1)S(1)}, bf16[8,2048]{1,0:T(8,128)(2,1)S(1)}, u32[]{:S(2)}, u32[]{:S(2)}) collective-permute-start(bf16[8,2048]{1,0:T(8,128)(2,1)S(1)} %slice.239), channel_id=1, source_target_pairs={{0,2},{2,4},{4,6},{1,3},{3,5},{5,7},{8,10},{10,12},{12,14},{9,11},... | collective-permute-start | bytes 98312 | tf_op jit(solution)/shard_map/ppermute | solution.py:17
  67.1 1.4 copy-start.10
  94.2 30.6 %copy-start.5 = (f32[264,2048]{1,0:T(8,128)S(1)}, f32[264,2048]{1,0:T(8,128)}, u32[]{:S(2)}) copy-start(f32[264,2048]{1,0:T(8,128)} %copy-done.4) | copy-start | bytes 6488068
  94.3 6.6 %collective-permute-start.3 = (f32[8,2048]{1,0:T(8,128)S(1)}, f32[8,2048]{1,0:T(8,128)S(1)}, u32[]{:S(2)}, u32[]{:S(2)}) collective-permute-start(f32[8,2048]{1,0:T(8,128)S(1)} %slice.249), channel_id=1, source_target_pairs={{2,0},{4,2},{6,4},{3,1},{5,3},{7,5},{10,8},{12,10},{14,12},{11,9},... | collective-permute-start | bytes 196616 | tf_op jit(solution)/shard_map/ppermute | solution.py:17
  101.0 23.8 %collective-permute-start.4 = (f32[256,2048]{1,0:T(8,128)S(1)}, f32[256,2048]{1,0:T(8,128)S(1)}, u32[]{:S(2)}, u32[]{:S(2)}) collective-permute-start(f32[256,2048]{1,0:T(8,128)S(1)} %slice_add_fusion.1), channel_id=1, source_target_pairs={{0,24},{8,0},{16,8},{24,16},{1,25},{9,1},{17,9},{25,17},{2,26},{10... | collective-permute-start | bytes 6291464 | tf_op jit(solution)/shard_map/ppermute | solution.py:23
  124.9 9.0 %copy-start.8 = (f32[256,2048]{1,0:T(8,128)}, f32[256,2048]{1,0:T(8,128)S(1)}, u32[]{:S(2)}) copy-start(f32[256,2048]{1,0:T(8,128)S(1)} %collective-permute-done.4) | copy-start | bytes 6291460
  130.3 3.6 %copy-start.7 = (f32[264,2048]{1,0:T(8,128)S(1)}, f32[264,2048]{1,0:T(8,128)}, u32[]{:S(2)}) copy-start(f32[264,2048]{1,0:T(8,128)} %copy-done.6) | copy-start | bytes 6488068
  132.1 2.2 %copy-start.1 = (f32[264,2048]{1,0:T(8,128)S(1)}, f32[264,2048]{1,0:T(8,128)}, u32[]{:S(2)}) copy-start(f32[264,2048]{1,0:T(8,128)} %copy-done) | copy-start | bytes 6488068
  132.1 2.7 %copy-start.3 = (bf16[1,256,2048]{2,1,0:T(8,128)(2,1)S(1)}, bf16[1,256,2048]{2,1,0:T(8,128)(2,1)}, u32[]{:S(2)}) copy-start(bf16[1,256,2048]{2,1,0:T(8,128)(2,1)} %param.5) | copy-start | bytes 3145732
  143.7 7.8 %copy-start.9 = (f32[256,2048]{1,0:T(8,128)S(1)}, f32[256,2048]{1,0:T(8,128)}, u32[]{:S(2)}) copy-start(f32[256,2048]{1,0:T(8,128)} %copy-done.8) | copy-start | bytes 6291460
  143.7 7.8 %copy-start.20 = (f32[264]{0:T(512)S(1)}, f32[264]{0:T(512)}, u32[]{:S(2)}) copy-start(f32[264]{0:T(512)} %get-tuple-element.69) | copy-start | bytes 3172
  151.4 5.1 %copy-start.12 = (f32[2048]{0:T(1024)S(1)}, f32[2048]{0:T(1024)}, u32[]{:S(2)}) copy-start(f32[2048]{0:T(1024)} %get-tuple-element.12) | copy-start | bytes 24580
  151.5 5.1 %copy-start.13 = (f32[2048]{0:T(1024)S(1)}, f32[2048]{0:T(1024)}, u32[]{:S(2)}) copy-start(f32[2048]{0:T(1024)} %get-tuple-element.13) | copy-start | bytes 24580
  151.5 5.1 %copy-start.14 = (f32[2048]{0:T(1024)S(1)}, f32[2048]{0:T(1024)}, u32[]{:S(2)}) copy-start(f32[2048]{0:T(1024)} %get-tuple-element.14) | copy-start | bytes 24580
  151.5 5.1 %copy-start.15 = (f32[2048]{0:T(1024)S(1)}, f32[2048]{0:T(1024)}, u32[]{:S(2)}) copy-start(f32[2048]{0:T(1024)} %get-tuple-element.15) | copy-start | bytes 24580
  151.5 5.1 %copy-start.16 = (f32[2048]{0:T(1024)S(1)}, f32[2048]{0:T(1024)}, u32[]{:S(2)}) copy-start(f32[2048]{0:T(1024)} %get-tuple-element.16) | copy-start | bytes 24580
  151.5 5.1 %copy-start.17 = (f32[2048]{0:T(1024)S(1)}, f32[2048]{0:T(1024)}, u32[]{:S(2)}) copy-start(f32[2048]{0:T(1024)} %get-tuple-element.30) | copy-start | bytes 24580
  151.5 5.1 %copy-start.18 = (f32[2048]{0:T(1024)S(1)}, f32[2048]{0:T(1024)}, u32[]{:S(2)}) copy-start(f32[2048]{0:T(1024)} %get-tuple-element.31) | copy-start | bytes 24580
  151.5 5.1 %copy-start.19 = (f32[2048]{0:T(1024)S(1)}, f32[2048]{0:T(1024)}, u32[]{:S(2)}) copy-start(f32[2048]{0:T(1024)} %get-tuple-element.32) | copy-start | bytes 24580
  153.8 1.4 copy-start.11
  155.2 6.8 %collective-permute-start.5 = (f32[8,2048]{1,0:T(8,128)S(1)}, f32[8,2048]{1,0:T(8,128)S(1)}, u32[]{:S(2)}, u32[]{:S(2)}) collective-permute-start(f32[8,2048]{1,0:T(8,128)S(1)} %slice.251), channel_id=1, source_target_pairs={{2,0},{4,2},{6,4},{3,1},{5,3},{7,5},{10,8},{12,10},{14,12},{11,9},... | collective-permute-start | bytes 196616 | tf_op jit(solution)/shard_map/ppermute | solution.py:17
Sparse Core Ops, SparseCore 0:
  157.8 22.3 reduce-scatter.1
